TPU v7x, 256 devices: a whole 4x4x8 slice. The times are simulated.
256 devices in a mesh: dp: 32 (over z, x), ctx: 8 (over y, core).
Axes of the slice: x: 4, y: 4, z: 8, core: 2. Of those that a mesh axis runs over, the one named last changes fastest.
Arguments:
- tokens: bfloat16 [32768, 8192], P(('dp', 'ctx')), may hold values from -24 to 24
- qkv: bfloat16 [32768, 1280], P(('dp', 'ctx')), may hold values from -8 to 8
- grad_out: bfloat16 [32768, 1024], P(('dp', 'ctx')), may hold values from -6 to 6
- span_order: int32 [32, 16], P('dp'), may hold values from 0 to 15, each once within a row
Outputs:
- grad_weight: float32 [8192, 1280], P(('dp', 'ctx'))
Inputs may be any that keep to these rules, and one draw needn't show every extreme that they name: Each row of span_order is a permutation of 0 to 15.
All inputs are finite; a program needn't handle non-finite values.
Results may differ from a plain program's by a relative error of at most 0.023.
Values may be sent and summed in bfloat16 or wider, within the bound.
A program may use at most 64 MiB of HBM per device.

v0:
```python
import math

import jax
import jax.numpy as jnp
from jax import lax
from jax.sharding import PartitionSpec as P

HEADS = 8
HD = 128


theta_base = 500000.0


def angles(positions, width):
    half = width // 2
    freq = jnp.exp(
        -(jnp.arange(half, dtype=jnp.float32) * 2.0 / width) * jnp.log(jnp.float32(theta_base))
    )
    turn = positions.astype(jnp.float32)[:, None] * freq[None, :]
    return (jnp.cos(turn), jnp.sin(turn))


def rotate(values, cosine, sine):
    half = values.shape[-1] // 2
    first = values[..., :half]
    second = values[..., half:]
    return jnp.concatenate(
        [first * cosine - second * sine, second * cosine + first * sine], axis=-1
    )


def rotate_back(grads, cosine, sine):
    half = grads.shape[-1] // 2
    first = grads[..., :half]
    second = grads[..., half:]
    return jnp.concatenate(
        [first * cosine + second * sine, second * cosine - first * sine], axis=-1
    )


def term_maker(source, grads_qkv):
    return lax.dot_general(
        source, grads_qkv, (((0,), (0,)), ((), ())), preferred_element_type=jnp.float32
    )


def body(tokens, qkv, grad_out, span_order):
    tdev, width = tokens.shape
    qwidth = HEADS * HD
    nctx = lax.axis_size("ctx")
    me = lax.axis_index("ctx")
    block = tdev // 2
    scale = 1.0 / math.sqrt(HD)
    offsets = jnp.arange(block, dtype=jnp.int32)
    key_pos = (span_order[0][:, None] * block + offsets[None, :]).reshape(-1)
    my_pos = lax.dynamic_slice_in_dim(key_pos, me * tdev, tdev)
    cosine, sine = angles(my_pos, HD)
    proj = qkv.astype(jnp.float32)
    rows = HEADS * tdev
    queries = proj[:, :qwidth].reshape(tdev, HEADS, HD).transpose(1, 0, 2)
    queries = rotate(queries, cosine, sine).astype(jnp.bfloat16).reshape(rows, HD)
    keys_own = rotate(proj[:, qwidth : qwidth + HD], cosine, sine).astype(jnp.bfloat16)
    values_own = qkv[:, qwidth + HD :]
    keys, values = (
        lax.all_gather(keys_own, "ctx", axis=0, tiled=True),
        lax.all_gather(values_own, "ctx", axis=0, tiled=True),
    )
    query_pos = jnp.tile(my_pos, HEADS)
    latest = jnp.max(my_pos)
    upstream = grad_out.reshape(tdev, HEADS, HD).transpose(1, 0, 2).reshape(rows, HD)
    upstream_f = upstream.astype(jnp.float32)
    flags = []
    key_tiles = []
    value_tiles = []
    score_tiles = []
    for shard in range(nctx):
        low = shard * tdev
        key_tile = keys[low : low + tdev]
        value_tiles.append(values[low : low + tdev])
        key_tiles.append(key_tile)
        tile_pos = key_pos[low : low + tdev]
        seen = jnp.min(tile_pos) <= latest
        flags.append(seen)

        def score(key_tile=key_tile, tile_pos=tile_pos):
            raw = (
                lax.dot_general(
                    queries, key_tile, (((1,), (1,)), ((), ())), preferred_element_type=jnp.float32
                )
                * scale
            )
            return jnp.where(tile_pos[None, :] <= query_pos[:, None], raw, -jnp.inf)

        score_tiles.append(score())
    peak = score_tiles[0].max(axis=1)
    for tile in score_tiles[1:]:
        peak = jnp.maximum(peak, tile.max(axis=1))
    exp_tiles = [jnp.exp(tile - peak[:, None]) for tile in score_tiles]
    denom = exp_tiles[0].sum(axis=1)
    for tile in exp_tiles[1:]:
        denom = denom + tile.sum(axis=1)
    prob_tiles = [tile / denom[:, None] for tile in exp_tiles]
    prob_b_tiles = [tile.astype(jnp.bfloat16) for tile in prob_tiles]
    empty_rows = jnp.zeros((rows, HD), jnp.float32)
    output = empty_rows
    for shard in range(nctx):

        def weighted(pb=prob_b_tiles[shard], vt=value_tiles[shard]):
            return jnp.dot(pb, vt, preferred_element_type=jnp.float32)

        output = output + weighted()
    delta = jnp.sum(upstream_f * output, axis=1)
    dq = empty_rows
    key_grad_tiles = []
    value_grad_tiles = []
    for shard in range(nctx):

        def backward(
            pt=prob_tiles[shard], pb=prob_b_tiles[shard], kt=key_tiles[shard], vt=value_tiles[shard]
        ):
            dprobs = lax.dot_general(
                upstream, vt, (((1,), (1,)), ((), ())), preferred_element_type=jnp.float32
            )
            dscores = (pt * (dprobs - delta[:, None])).astype(jnp.bfloat16)
            dq_part = jnp.dot(dscores, kt, preferred_element_type=jnp.float32)
            dk_part = lax.dot_general(
                dscores, queries, (((0,), (0,)), ((), ())), preferred_element_type=jnp.float32
            )
            dv_part = lax.dot_general(
                pb, upstream, (((0,), (0,)), ((), ())), preferred_element_type=jnp.float32
            )
            return (dq_part, dk_part, dv_part)

        dq_part, dk_part, dv_part = backward()
        dq = dq + dq_part
        key_grad_tiles.append(dk_part)
        value_grad_tiles.append(dv_part)
    key_grads = jnp.concatenate(key_grad_tiles, axis=0)
    value_grads = jnp.concatenate(value_grad_tiles, axis=0)
    summed_keys, summed_values = (
        lax.psum(key_grads.astype(jnp.bfloat16), "ctx").astype(jnp.float32),
        lax.psum(value_grads.astype(jnp.bfloat16), "ctx").astype(jnp.float32),
    )
    own_keys = lax.dynamic_slice_in_dim(summed_keys, me * tdev, tdev)
    own_values = lax.dynamic_slice_in_dim(summed_values, me * tdev, tdev)
    dq_rows = (
        rotate_back((dq * scale).reshape(HEADS, tdev, HD), cosine, sine)
        .transpose(1, 0, 2)
        .reshape(tdev, qwidth)
    )
    dk_rows = rotate_back(own_keys * scale, cosine, sine)
    grads_qkv = jnp.concatenate([dq_rows, dk_rows, own_values], axis=1).astype(jnp.bfloat16)
    share = lax.psum_scatter(
        term_maker(tokens, grads_qkv).astype(jnp.bfloat16), "dp", scatter_dimension=0, tiled=True
    )
    result = lax.psum_scatter(share, "ctx", scatter_dimension=0, tiled=True).astype(jnp.float32)
    return result


def solution(mesh):
    return jax.shard_map(
        body,
        mesh=mesh,
        in_specs=(
            P(("dp", "ctx"), None),
            P(("dp", "ctx"), None),
            P(("dp", "ctx"), None),
            P("dp", None),
        ),
        out_specs=P(("dp", "ctx"), None),
        check_vma=False,
    )
```

profile of v0, /device:TPU:1, one launch (start us, length us, event | category | flops | bytes accessed | tf_op | source)
XLA Modules:
  0.0 433.9 jit_solution(13742520347430512591)
XLA Ops:
  6.6 0.8 multiply_bitcast_fusion
  7.5 1.2 copy.107
  8.8 0.9 convert_element_type.78
  10.4 15.9 %all_gather.7 = bf16[1024,128]{1,0:T(8,128)(2,1)S(1)} all-gather(bf16[128,128]{1,0:T(8,128)(2,1)S(1)} %slice-done), channel_id=1, replica_groups=mesh['dp'=32,'ctx'=8] {'ctx'}, dimensions={0}, use_global_device_ids=true | all-gather | bytes 294912 | tf_op jit(solution)/shard_map/all_gather | solution.py:67
  26.3 0.9 copy.110
  27.2 1.0 fusion.103
  28.2 11.5 %all_gather.6 = bf16[1024,128]{0,1:T(8,128)(2,1)S(1)} all-gather(bf16[128,128]{0,1:T(8,128)(2,1)S(1)} %pad_maximum_fusion.1), channel_id=1, replica_groups=mesh['dp'=32,'ctx'=8] {'ctx'}, dimensions={0}, use_global_device_ids=true | all-gather | bytes 294912 | tf_op jit(solution)/shard_map/all_gather | solution.py:66
  39.9 0.3 fusion.180
  40.2 0.3 fusion.181
  40.5 0.3 fusion.182
  40.8 0.3 fusion.183
  41.0 0.3 fusion.184
  41.3 0.3 fusion.185
  41.6 0.3 fusion.187
  41.9 0.3 fusion.186
  42.2 0.6 fusion.48
  42.9 0.3 copy-done.11
  43.4 0.3 fusion.124
  43.7 0.3 convolution_add_fusion.13
  44.0 0.3 convolution_add_fusion.12
  44.3 0.3 convolution_add_fusion.11
  44.5 0.3 convolution_add_fusion.10
  44.8 0.3 convolution_add_fusion.9
  45.1 0.3 convolution_add_fusion.8
  45.4 0.3 fusion.28
  46.4 1.1 fusion.23
  48.7 0.3 fusion.34
  48.9 0.3 fusion.33
  49.5 0.3 fusion.31
  49.7 0.3 fusion.30
  50.3 0.9 fusion.44
  51.1 0.9 fusion.43
  52.0 0.8 fusion.42
  52.9 0.8 fusion.41
  53.7 0.9 fusion.40
  54.6 0.9 fusion.39
  55.4 0.9 fusion.38
  56.3 0.9 fusion.37
  57.5 1.0 fusion.141
  58.5 1.2 convolution_add_fusion.6
  61.4 60.7 %all-reduce.3.cloned.1.call-done = (bf16[1024,128]{1,0:T(8,128)(2,1)}, bf16[1024,128]{0,1:T(8,128)(2,1)}) async-done(((bf16[1024,128]{1,0:T(8,128)(2,1)}, bf16[1024,128]{0,1:T(8,128)(2,1)}), (bf16[1024,128]{1,0:T(8,128)(2,1)}, bf16[1024,128]{0,1:T(8,128)(2,1)})) %all-reduce.3.cloned.1.call-update) | async-done | bytes 524304 | tf_op jit(solution)/shard_map/psum | solution.py:143
  122.1 0.8 convert_convert_fusion
  122.9 0.8 convert_multiply_fusion
  124.0 9.9 %fusion = bf16[8192,1280]{0,1:T(8,128)(2,1)} fusion(bf16[128,8192]{1,0:T(8,128)(2,1)S(1)} %copy-done, bf16[128,128]{0,1:T(8,128)(2,1)S(1)} %copy.137, bf16[128,64]{0,1:T(8,128)(2,1)S(1)} %get-tuple-element.26, bf16[128,64]{0,1:T(8,128)(2,1)S(1)} %get-tuple-element.25, bf16[128,1024]{0,1:T(8,128)(2,1)S(1)} %bitcast.101), kind=kOutput, calls=%fused_computation.1 | convolution fusion | flops 2696151040 | bytes 23396352 | tf_op jit(solution)/shard_map/dot_general | solution.py:43
  134.0 255.3 %reduce-scatter.5.cloned.1.call-done = bf16[256,1280]{0,1:T(8,128)(2,1)} async-done(((bf16[8192,1280]{0,1:T(8,128)(2,1)}), bf16[256,1280]{0,1:T(8,128)(2,1)}) %reduce-scatter.5.cloned.1.call-update) | async-done | bytes 655376 | tf_op jit(solution)/shard_map/reduce_scatter | solution.py:154
  389.3 2.2 copy.163
  391.5 34.3 %reduce-scatter.7.cloned.1.call-done = bf16[32,1280]{1,0:T(8,128)(2,1)} async-done(((bf16[256,1280]{1,0:T(8,128)(2,1)}), bf16[32,1280]{1,0:T(8,128)(2,1)}) %reduce-scatter.7.cloned.1.call-update) | async-done | bytes 81936 | tf_op jit(solution)/shard_map/reduce_scatter | solution.py:157
  425.8 1.6 convert_element_type.101
  (78 shorter events, 5.9 us)
Async XLA Ops:
  6.5 117.4 %copy-start = (bf16[128,8192]{1,0:T(8,128)(2,1)S(1)}, bf16[128,8192]{1,0:T(8,128)(2,1)}, u32[]{:S(2)}) copy-start(bf16[128,8192]{1,0:T(8,128)(2,1)} %param.4) | copy-start | bytes 6291460
  6.5 3.8 slice-start
  6.5 19.7 %copy-start.10 = (bf16[128,1024]{1,0:T(8,128)(2,1)S(1)}, bf16[128,1024]{1,0:T(8,128)(2,1)}, u32[]{:S(2)}) copy-start(bf16[128,1024]{1,0:T(8,128)(2,1)} %param.6) | copy-start | bytes 786436
  6.5 115.6 %all-reduce.3.cloned.1.call-start = ((), (), s32[]{:S(2)}) async-start(), calls=%async_computation.4 | async-start | bytes 1048576 | tf_op jit(solution)/shard_map/psum | solution.py:143
  26.2 19.9 %copy-start.8 = (bf16[1024,128]{1,0:T(8,128)(2,1)}, bf16[1024,128]{1,0:T(8,128)(2,1)S(1)}, u32[]{:S(2)}) copy-start(bf16[1024,128]{1,0:T(8,128)(2,1)S(1)} %all_gather.7) | copy-start | bytes 786436
  39.7 3.7 copy-start.6
  42.2 1.0 copy-start.11
  45.9 5.3 %copy-start.5 = (bf16[1024,128]{0,1:T(8,128)(2,1)}, bf16[1024,128]{0,1:T(8,128)(2,1)S(1)}, u32[]{:S(2)}) copy-start(bf16[1024,128]{0,1:T(8,128)(2,1)S(1)} %fusion.26) | copy-start | bytes 786436
  46.1 5.9 %copy-start.3 = (bf16[1024,128]{0,1:T(8,128)(2,1)}, bf16[1024,128]{0,1:T(8,128)(2,1)S(1)}, u32[]{:S(2)}) copy-start(bf16[1024,128]{0,1:T(8,128)(2,1)S(1)} %fusion.25) | copy-start | bytes 786436
  46.4 6.5 %copy-start.1 = (bf16[1024,128]{0,1:T(8,128)(2,1)}, bf16[1024,128]{0,1:T(8,128)(2,1)S(1)}, u32[]{:S(2)}) copy-start(bf16[1024,128]{0,1:T(8,128)(2,1)S(1)} %fusion.24) | copy-start | bytes 786436
  46.4 1.1 copy-start.9
  50.3 3.5 copy-start.12
  57.2 332.1 %reduce-scatter.5.cloned.1.call-start = ((), (), s32[]{:S(2)}) async-start(), calls=%async_computation.2 | async-start | bytes 21626880 | tf_op jit(solution)/shard_map/reduce_scatter | solution.py:154
  57.4 2.3 copy-start.4
  57.4 2.3 copy-start.7
  57.5 2.5 copy-start.2
  133.9 291.8 %reduce-scatter.7.cloned.1.call-start = ((), (), s32[]{:S(2)}) async-start(), calls=%async_computation.3 | async-start | bytes 737280 | tf_op jit(solution)/shard_map/reduce_scatter | solution.py:157
Sparse Core Ops, SparseCore 0:
  57.3 64.7 all-reduce.2
  134.1 255.1 reduce-scatter.4
  391.8 33.9 reduce-scatter.6
where the time goes:
time: 436 us; the launch traced here: 434 us
  waiting for transfers between devices  350 us (80%)
  matrix products  29.5 us (7%)
  blocking collectives  27.4 us (6%)
  between operations  13.7 us (3%)
  other arithmetic  6.97 us (2%)
  local copies, waits for them, and re-layouts  5.72 us (1%)
    reduce_scatter x1, waiting for transfers between devices, body(): lax.psum_scatter(term_maker(tokens, grads_qkv).astype(jnp.bfloat16), 'dp'...  255 us
    psum x1, waiting for transfers between devices, body(): lax.psum(value_grads.astype(jnp.bfloat16), 'ctx').astype(jnp.float32)  60.7 us
    reduce_scatter x1, waiting for transfers between devices, body(): lax.psum_scatter(share, 'ctx', scatter_dimension=0, tiled=True)  34.3 us
    all_gather x1, blocking collectives, body(): lax.all_gather(values_own, 'ctx', axis=0, tiled=True)  15.9 us
    all_gather x1, blocking collectives, body(): lax.all_gather(keys_own, 'ctx', axis=0, tiled=True)  11.5 us
    dot_general x1, matrix products, term_maker(): lax.dot_general(source, grads_qkv, (((0,), (0,)), ((), ())), preferred_el...  9.93 us
  transfers between devices with their start and end apart: 3, of which 3 were waited for; matrix products, arithmetic and copies ran while one was open for 1% of the time, Pallas kernels for 0%

commit v1 on v0

v1 whole, which is shorter than its diff:
```python
import functools
import math

import jax
import jax.numpy as jnp
from jax import lax
from jax.experimental import pallas as pl
from jax.experimental.pallas import tpu as pltpu
from jax.sharding import PartitionSpec as P

HEADS = 8
HD = 128
TDEV = 128
SEQ = 1024
QW = HEADS * HD
NX = 4
NZ = 8
SPAN = 64
SPANS = 16
LOG_BASE = math.log(500000.0)
SCALE = 1.0 / math.sqrt(HD)
LOG2E = 1.4426950408889634
MESH = pl.DeviceIdType.MESH
BF = jnp.bfloat16
F32 = jnp.float32
CHUNKS = ((0, 512), (512, 512), (1024, 256))
LAGS = (0, 0, 1)


def kernel(
    tok_h, qkv_h, go_h, span_s, out_ref,
    tokv, qkvv, gov, q_s, g_s, kv, bias, cos_s, sin_s, dkt, dvt, dsend, drecv,
    tr, at, bq_own, bk_own, bq, bk, y1s, y1r, y2s, y2r, cacc, zs, zr,
    lsem, kvs, kvr, asnd, arcv, dss, dsr, bs, br, cs, cr,
):
    dp = lax.axis_index("dp")
    ctx = lax.axis_index("ctx")
    z = dp // NX
    x = dp % NX
    y = ctx // 2
    c = ctx % 2

    def dev(zz, xx, yy, cc):
        return (zz * NX + xx, yy * 2 + cc)

    def rcopy(src, dst, ssem, rsem, to):
        return pltpu.make_async_remote_copy(
            src_ref=src, dst_ref=dst, send_sem=ssem, recv_sem=rsem,
            device_id=to, device_id_type=MESH,
        )

    pending = []

    def send(src, dst, ssem, rsem, to):
        copy = rcopy(src, dst, ssem, rsem, to)
        copy.start()
        pending.append(copy)

    partner = dev(z, x, y, 1 - c)

    def got(dst, sem):
        rcopy(dst, dst, kvs.at[0], sem, partner).wait_recv()

    loads = [
        pltpu.make_async_copy(qkv_h, qkvv, lsem.at[0]),
        pltpu.make_async_copy(go_h, gov, lsem.at[1]),
        pltpu.make_async_copy(tok_h, tokv, lsem.at[2]),
    ]
    for load in loads:
        load.start()

    barrier = pltpu.get_barrier_semaphore()
    peers = [partner]
    for off in range(1, NX):
        for cc in range(2):
            peers.append(dev(z, x, (y + off) % NX, cc))
            peers.append(dev(z, (x + off) % NX, y, cc))
    peers.append(dev((z + 1) % NZ, x, y, c))
    peers.append(dev((z + NZ - 1) % NZ, x, y, c))
    for peer in peers:
        pl.semaphore_signal(barrier, inc=1, device_id=peer, device_id_type=MESH)

    rows = lax.broadcasted_iota(jnp.int32, (TDEV, HD), 0)
    lanes = lax.broadcasted_iota(jnp.int32, (TDEV, HD), 1)
    first = span_s[0, 2 * ctx]
    second = span_s[0, 2 * ctx + 1]
    pos = jnp.where(rows < SPAN, first * SPAN + rows, second * SPAN + rows - SPAN)
    half = (lanes % (HD // 2)).astype(F32)
    freq = jnp.exp(half * (-2.0 / HD) * jnp.float32(LOG_BASE))
    angle = pos.astype(F32) * freq
    cosine = jnp.cos(angle)
    sine = jnp.sin(angle)
    sine = jnp.where(lanes < HD // 2, -sine, sine)
    cos_s[...] = cosine
    sin_s[...] = sine

    def rot(a):
        return a * cosine + pltpu.roll(a, HD // 2, 1) * sine

    loads[0].wait()
    kv_rows = pl.ds(pl.multiple_of(ctx * TDEV, TDEV), TDEV)
    kv[kv_rows, :HD] = rot(qkvv[:, QW:QW + HD].astype(F32)).astype(BF)
    kv[kv_rows, HD:] = qkvv[:, QW + HD:]

    pl.semaphore_wait(barrier, len(peers))

    own_kv = kv.at[kv_rows, :]
    for off in range(1, NX):
        send(own_kv, own_kv, kvs.at[off - 1], kvr.at[off - 1], dev(z, x, (y + off) % NX, c))
    send(own_kv, own_kv, kvs.at[3], kvr.at[3], partner)

    loads[2].wait()

    def turn(zz, carry):
        for xx in range(NX):
            block = tokv[:, pl.ds(pl.multiple_of(zz * 1024 + xx * 256, 256), 256)]
            flip = block.T
            for yy in range(NX):
                at_row = pl.multiple_of(zz * 32, 32)
                tr[0, xx, pl.ds(yy * 256 + at_row, 32), :] = flip[yy * 64:yy * 64 + 32]
                tr[1, yy, pl.ds(xx * 256 + at_row, 32), :] = flip[yy * 64 + 32:yy * 64 + 64]
        return carry

    lax.fori_loop(0, NZ, turn, 0)

    def slot(m):
        return pl.ds(pl.multiple_of(m * TDEV, TDEV), TDEV)

    gpos = x * (1 - c) + y * c
    opos = y * (1 - c) + x * c
    mine = slot(gpos * 2 + c)
    for off in (2, 1, 3):
        to_x = (x + off) % NX
        to_y = (y + off) % NX
        send(tr.at[0, to_x], at.at[:, slot(x * 2 + c)],
             asnd.at[off - 1], arcv.at[(off - 1) * 2 + c], dev(z, to_x, y, 0))
        send(tr.at[1, to_y], at.at[:, slot(y * 2 + c)],
             asnd.at[off + 2], arcv.at[(off - 1) * 2 + c], dev(z, x, to_y, 1))
    send(tr.at[1 - c, opos], at.at[:, slot(opos * 2 + c)], asnd.at[6], arcv.at[6], partner)
    own_a = pltpu.make_async_copy(tr.at[c, gpos], at.at[:, mine], lsem.at[3])
    own_a.start()

    for h in range(HEADS):
        q_s[h * TDEV:(h + 1) * TDEV, :] = rot(
            qkvv[:, h * HD:(h + 1) * HD].astype(F32)).astype(BF)
    loads[1].wait()
    for h in range(HEADS):
        g_s[h * TDEV:(h + 1) * TDEV, :] = gov[:, h * HD:(h + 1) * HD]
    key = lax.broadcasted_iota(jnp.int32, (1, SEQ), 1)
    key_span = key // SPAN
    key_pos = key % SPAN
    for i in range(SPANS):
        key_pos = key_pos + jnp.where(key_span == i, span_s[0, i] * SPAN, 0)
    masked = jnp.where(key_pos <= pos[:, :1], jnp.float32(0.0), jnp.float32(-1e30))
    bias[:TDEV, :] = masked
    bias[TDEV:, :] = masked
    dkt[...] = jnp.zeros_like(dkt)
    dvt[...] = jnp.zeros_like(dvt)

    for off in (1, 3, 2):
        rows_in = slot(((y + NX - off) % NX) * 2 + c)
        got(kv.at[rows_in, :], kvr.at[off - 1])
        send(kv.at[rows_in, :], kv.at[rows_in, :], kvs.at[3 + off], kvr.at[3 + off], partner)
    got(own_kv, kvr.at[3])
    for off in (1, 3, 2):
        got(own_kv, kvr.at[3 + off])

    def heads(i, carry):
        two = pl.ds(pl.multiple_of(i * 2 * TDEV, 2 * TDEV), 2 * TDEV)
        q2 = q_s[two, :]
        g2 = g_s[two, :]
        keys = kv[:, :HD]
        values = kv[:, HD:]
        s = lax.dot_general(q2, keys, (((1,), (1,)), ((), ())), preferred_element_type=F32)
        s = s * jnp.float32(SCALE * LOG2E) + bias[...]
        e = jnp.exp2(s - jnp.max(s, axis=1, keepdims=True))
        p = e * (1.0 / jnp.sum(e, axis=1, keepdims=True))
        pb = p.astype(BF)
        o = jnp.dot(pb, values, preferred_element_type=F32)
        delta = jnp.sum(g2.astype(F32) * o, axis=1, keepdims=True)
        dpr = lax.dot_general(g2, values, (((1,), (1,)), ((), ())), preferred_element_type=F32)
        ds = (p * (dpr - delta)).astype(BF)
        dq = jnp.dot(ds, keys, preferred_element_type=F32) * jnp.float32(SCALE)
        for j in range(2):
            g = dq[j * TDEV:(j + 1) * TDEV]
            back = g * cos_s[...] - pltpu.roll(g, HD // 2, 1) * sin_s[...]
            at_col = pl.multiple_of((2 * i + j) * HD, HD)
            bq_own[:, pl.ds(at_col, HD)] = back.astype(BF)
        dkt[...] += lax.dot_general(q2, ds, (((0,), (0,)), ((), ())), preferred_element_type=F32)
        dvt[...] += lax.dot_general(g2, pb, (((0,), (0,)), ((), ())), preferred_element_type=F32)
        return carry

    lax.fori_loop(0, HEADS // 2, heads, 0)

    for j in range(8):
        dsend[j, :HD, :] = dkt[:, j * TDEV:(j + 1) * TDEV].astype(BF)
        dsend[j, HD:, :] = dvt[:, j * TDEV:(j + 1) * TDEV].astype(BF)
    for off in range(1, 8):
        to = (ctx + off) % 8
        send(dsend.at[to], drecv.at[off - 1], dss.at[off - 1], dsr.at[off - 1], (dp, to))

    def spread(own, group, base, sem):
        for k, off in enumerate((1, NX - 1)):
            send(own, group.at[slot(x * 2 + c), :], bs.at[base + k],
                 br.at[base + 2 * k + c], dev(z, (x + off) % NX, y, 0))
            send(own, group.at[slot(y * 2 + c), :], bs.at[base + 2 + k],
                 br.at[base + 2 * k + c], dev(z, x, (y + off) % NX, 1))
        send(own, group.at[slot(opos * 2 + c), :], bs.at[base + 4], br.at[base + 6], partner)
        copy = pltpu.make_async_copy(own, group.at[mine, :], sem)
        copy.start()
        return copy

    def beside(step):
        return dev(z, (x + (1 - c) * step) % NX, (y + c * step) % NX, c)

    below = (gpos + NX - 1) % NX
    above = (gpos + 1) % NX

    def relay(group, base):
        up = group.at[slot(below * 2), :]
        got(up, br.at[base])
        send(up, up, bs.at[base + 5], br.at[base + 4], beside(1))
        down = group.at[slot(above * 2 + 1), :]
        got(down, br.at[base + 3])
        send(down, down, bs.at[base + 6], br.at[base + 5], beside(NX - 1))

    def rest(group, base, local):
        local.wait()
        for k in (1, 2, 4, 5, 6):
            got(group.at[mine, :], br.at[base + k])

    copy_q = spread(bq_own, bq, 0, lsem.at[4])
    relay(bq, 0)

    own_cols = pl.ds(pl.multiple_of(ctx * TDEV, TDEV), TDEV)
    for off in range(1, 8):
        got(drecv.at[off - 1], dsr.at[off - 1])
    dk = dkt[:, own_cols]
    dv = dvt[:, own_cols]
    for off in range(1, 8):
        dk = dk + drecv[off - 1, :HD, :].astype(F32)
        dv = dv + drecv[off - 1, HD:, :].astype(F32)
    dk = dk.T * jnp.float32(SCALE)
    bk_own[:, :HD] = (dk * cos_s[...] - pltpu.roll(dk, HD // 2, 1) * sin_s[...]).astype(BF)
    bk_own[:, HD:] = dv.T.astype(BF)
    copy_k = spread(bk_own, bk, 7, lsem.at[5])
    relay(bk, 7)

    own_a.wait()
    for k in range(7):
        got(at.at[:, mine], arcv.at[k])
    rest(bq, 0, copy_q)

    def across(step):
        return dev(z, (x + c * step) % NX, (y + (1 - c) * step) % NX, c)

    up_dev, down_dev = across(1), across(NX - 1)
    zup_dev, zdown_dev = dev((z + 1) % NZ, x, y, c), dev((z + NZ - 1) % NZ, x, y, c)

    def term(a, ch):
        first_col, width = CHUNKS[ch]
        lhs = at[pl.ds(pl.multiple_of(a * 256, 256), 256), :]
        if first_col < QW:
            rhs = bq[:, first_col:first_col + width]
        else:
            rhs = bk[:, first_col - QW:first_col - QW + width]
        return jnp.dot(lhs, rhs, preferred_element_type=F32)

    def zrows(zz):
        return pl.multiple_of(zz * 32, 32)

    def stage(ch, s):
        first_col, width = CHUNKS[ch]
        cols = slice(first_col, first_col + width)
        base = ch * 12
        if s == 0:
            y1s[:, cols] = term((opos + 2) % NX, ch).astype(BF)
            send(y1s.at[:128, cols], y1r.at[0, :, cols], cs.at[base], cr.at[base], up_dev)
            send(y1s.at[128:, cols], y1r.at[1, :, cols], cs.at[base + 1], cr.at[base + 1], down_dev)
        elif s == 1:
            t = term((opos + 1) % NX, ch)
            got(y1r.at[0, :, cols], cr.at[base])
            y2s[0, :128, cols] = (t[:128] + y1r[0, :, cols].astype(F32)).astype(BF)
            y2s[0, 128:, cols] = t[128:].astype(BF)
            send(y2s.at[0, :, cols], y2r.at[0, :, cols], cs.at[base + 2], cr.at[base + 2], up_dev)
            t = term((opos + NX - 1) % NX, ch)
            got(y1r.at[1, :, cols], cr.at[base + 1])
            y2s[1, :128, cols] = t[:128].astype(BF)
            y2s[1, 128:, cols] = (t[128:] + y1r[1, :, cols].astype(F32)).astype(BF)
            send(y2s.at[1, :, cols], y2r.at[1, :, cols], cs.at[base + 3], cr.at[base + 3], down_dev)
        elif s == 2:
            cacc[:, cols] = term(opos, ch)
            got(y2r.at[0, :, cols], cr.at[base + 2])
            got(y2r.at[1, :, cols], cr.at[base + 3])
            cacc[:, cols] += y2r[0, :, cols].astype(F32) + y2r[1, :, cols].astype(F32)
            far = zrows((z + 4) % NZ)
            zs[0, 0, :16, cols] = cacc[pl.ds(far, 16), cols].astype(BF)
            zs[0, 1, :16, cols] = cacc[pl.ds(far + 16, 16), cols].astype(BF)
            for d, to in enumerate((zup_dev, zdown_dev)):
                send(zs.at[0, d, :16, cols], zr.at[0, d, :16, cols],
                     cs.at[base + 4 + d], cr.at[base + 4 + d], to)
        elif s < 6:
            k = s - 2
            for d, to in enumerate((zup_dev, zdown_dev)):
                step = 4 - k
                blk = zrows((z + (step if d == 0 else NZ - step)) % NZ)
                sem = base + 4 + 2 * (k - 1) + d
                if k == 1:
                    got(zr.at[0, d, :16, cols], cr.at[sem])
                    low = cacc[pl.ds(blk, 16), cols]
                    high = cacc[pl.ds(blk + 16, 16), cols]
                    came = zr[0, d, :16, cols].astype(F32)
                    if d == 0:
                        low = low + came
                    else:
                        high = high + came
                    zs[k, d, :16, cols] = low.astype(BF)
                    zs[k, d, 16:, cols] = high.astype(BF)
                else:
                    got(zr.at[k - 1, d, :, cols], cr.at[sem])
                    zs[k, d, :, cols] = (
                        cacc[pl.ds(blk, 32), cols] + zr[k - 1, d, :, cols].astype(F32)
                    ).astype(BF)
                send(zs.at[k, d, :, cols], zr.at[k, d, :, cols],
                     cs.at[sem + 2], cr.at[sem + 2], to)
        else:
            for d in range(2):
                got(zr.at[3, d, :, cols], cr.at[base + 10 + d])
            out_ref[:, cols] = (
                cacc[pl.ds(zrows(z), 32), cols]
                + zr[3, 0, :, cols].astype(F32) + zr[3, 1, :, cols].astype(F32)
            )

    have_k = False
    for t in range(7 + max(LAGS)):
        for ch in range(len(CHUNKS)):
            s = t - LAGS[ch]
            if 0 <= s <= 6:
                if CHUNKS[ch][0] >= QW and not have_k:
                    rest(bk, 7, copy_k)
                    have_k = True
                stage(ch, s)

    for copy in pending:
        copy.wait_send()


def body(tokens, qkv, grad_out, span_order):
    n_c = 12 * len(CHUNKS)
    dma = pltpu.SemaphoreType.DMA
    v = pltpu.VMEM
    return pl.pallas_call(
        kernel,
        out_shape=jax.ShapeDtypeStruct((32, 1280), F32),
        in_specs=[pl.BlockSpec(memory_space=pl.ANY)] * 3
        + [pl.BlockSpec(memory_space=pltpu.SMEM)],
        out_specs=pl.BlockSpec(memory_space=pltpu.VMEM),
        scratch_shapes=[
            v((TDEV, 8192), BF), v((TDEV, 1280), BF), v((TDEV, QW), BF),
            v((SEQ, HD), BF), v((SEQ, HD), BF), v((SEQ, 2 * HD), BF),
            v((2 * TDEV, SEQ), F32), v((TDEV, HD), F32), v((TDEV, HD), F32),
            v((HD, SEQ), F32), v((HD, SEQ), F32),
            v((8, 2 * HD, TDEV), BF), v((7, 2 * HD, TDEV), BF),
            v((2, NX, 1024, TDEV), BF), v((1024, SEQ), BF),
            v((TDEV, QW), BF), v((TDEV, 256), BF), v((SEQ, QW), BF), v((SEQ, 256), BF),
            v((256, 1280), BF), v((2, 128, 1280), BF),
            v((2, 256, 1280), BF), v((2, 256, 1280), BF),
            v((256, 1280), F32), v((4, 2, 32, 1280), BF), v((4, 2, 32, 1280), BF),
            dma((6,)), dma((7,)), dma((7,)), dma((7,)), dma((7,)), dma((7,)), dma((7,)),
            dma((14,)), dma((14,)), dma((n_c,)), dma((n_c,)),
        ],
        compiler_params=pltpu.CompilerParams(collective_id=0, has_side_effects=True),
    )(tokens, qkv, grad_out, span_order)


def solution(mesh):
    return jax.shard_map(
        body,
        mesh=mesh,
        in_specs=(
            P(("dp", "ctx"), None),
            P(("dp", "ctx"), None),
            P(("dp", "ctx"), None),
            P("dp", None),
        ),
        out_specs=P(("dp", "ctx"), None),
        check_vma=False,
    )
```

time: 436 us -> 76.3 us (0.17)
  the two profiles are of different devices: /device:TPU:1 before, /device:TPU:9 now
where the time goes in v1:
time: 76.3 us; the launch traced here: 76.1 us
  Pallas kernels  74.5 us (98%)
  local copies, waits for them, and re-layouts  1.59 us (2%)
    pallas_call x1, Pallas kernels, body(): pl.pallas_call(kernel, out_shape=jax.ShapeDtypeStruct((32, 1280), F32), i...  74.5 us
    unnamed x1, local copies, waits for them, and re-layouts  1.59 us

profile of v1, /device:TPU:9, one launch (start us, length us, event | category | flops | bytes accessed | tf_op | source)
XLA Modules:
  0.0 76.1 jit_solution(6295595859798667055)
XLA Ops:
  0.0 74.5 %shard_map.46 = f32[32,1280]{1,0:T(8,128)} custom-call(bf16[128,8192]{1,0:T(8,128)(2,1)} %tok_h.1, bf16[128,1280]{1,0:T(8,128)(2,1)} %qkv_h.1, bf16[128,1024]{1,0:T(8,128)(2,1)} %go_h.1, s32[1,16]{1,0:T(1,128)} %span_s.1), custom_call_target="tpu_custom_call" | custom-call | tf_op jit(solution)/shard_map/pallas_call | solution.py:352
  74.6 1.6 %copy.6 = f32[32,1280]{1,0:T(8,128)} copy(f32[32,1280]{1,0:T(8,128)} %shard_map.46) | data formatting | bytes 327680

commit v2 on v1

v2 whole, which is shorter than its diff:
```python
import functools
import math

import jax
import jax.numpy as jnp
from jax import lax
from jax.experimental import pallas as pl
from jax.experimental.pallas import tpu as pltpu
from jax.sharding import PartitionSpec as P

HEADS = 8
HD = 128
TDEV = 128
SEQ = 1024
QW = HEADS * HD
NX = 4
NZ = 8
SPAN = 64
SPANS = 16
LOG_BASE = math.log(500000.0)
SCALE = 1.0 / math.sqrt(HD)
LOG2E = 1.4426950408889634
MESH = pl.DeviceIdType.MESH
BF = jnp.bfloat16
F32 = jnp.float32
NQ = 2
PER = HEADS // NQ
QC = QW // NQ
WIDTHS = (QC,) * NQ + (2 * HD,)
STARTS = tuple(QC * i for i in range(NQ)) + (QW,)
NCH = NQ + 1
LAGS = (0, 1, 2)


def kernel(
    tok_h, qkv_h, go_h, span_s, out_ref,
    tokv, qkvv, gov, q_s, g_s, kv, bias, cos_s, sin_s, dkt, dvt, psend, precv, dsend, drecv,
    tr, at, bq_own, bk_own, bq, bk, y1s, y1r, y2s, y2r, cacc, zs, zr,
    lsem, kvs, kvr, asnd, arcv, dss, dsr, bs, br, cs, cr,
):
    dp = lax.axis_index("dp")
    ctx = lax.axis_index("ctx")
    z = dp // NX
    x = dp % NX
    y = ctx // 2
    c = ctx % 2

    def dev(zz, xx, yy, cc):
        return (zz * NX + xx, yy * 2 + cc)

    def rcopy(src, dst, ssem, rsem, to):
        return pltpu.make_async_remote_copy(
            src_ref=src, dst_ref=dst, send_sem=ssem, recv_sem=rsem,
            device_id=to, device_id_type=MESH,
        )

    pending = []

    def send(src, dst, ssem, rsem, to):
        copy = rcopy(src, dst, ssem, rsem, to)
        copy.start()
        pending.append(copy)

    partner = dev(z, x, y, 1 - c)

    def got(dst, sem):
        rcopy(dst, dst, kvs.at[0], sem, partner).wait_recv()

    loads = [
        pltpu.make_async_copy(qkv_h, qkvv, lsem.at[0]),
        pltpu.make_async_copy(go_h, gov, lsem.at[1]),
        pltpu.make_async_copy(tok_h, tokv, lsem.at[2]),
    ]
    for load in loads:
        load.start()

    barrier = pltpu.get_barrier_semaphore()
    peers = [dev((z + off) % NZ, x, y, c) for off in (1, 7, 2, 6)]
    for off in range(1, NX):
        for cc in range(2):
            peers.append(dev(z, x, (y + off) % NX, cc))
            peers.append(dev(z, (x + off) % NX, y, cc))
    peers.append(partner)
    for peer in peers:
        pl.semaphore_signal(barrier, inc=1, device_id=peer, device_id_type=MESH)

    rows = lax.broadcasted_iota(jnp.int32, (TDEV, HD), 0)
    lanes = lax.broadcasted_iota(jnp.int32, (TDEV, HD), 1)
    first = span_s[0, 2 * ctx]
    second = span_s[0, 2 * ctx + 1]
    pos = jnp.where(rows < SPAN, first * SPAN + rows, second * SPAN + rows - SPAN)
    half = (lanes % (HD // 2)).astype(F32)
    freq = jnp.exp(half * (-2.0 / HD) * jnp.float32(LOG_BASE))
    angle = pos.astype(F32) * freq
    cosine = jnp.cos(angle)
    sine = jnp.sin(angle)
    sine = jnp.where(lanes < HD // 2, -sine, sine)
    cos_s[...] = cosine
    sin_s[...] = sine

    def rot(a):
        return a * cosine + pltpu.roll(a, HD // 2, 1) * sine

    loads[0].wait()
    kv_rows = pl.ds(pl.multiple_of(ctx * TDEV, TDEV), TDEV)
    kv[kv_rows, :HD] = rot(qkvv[:, QW:QW + HD].astype(F32)).astype(BF)
    kv[kv_rows, HD:] = qkvv[:, QW + HD:]

    loads[2].wait()

    def turn(zz, carry):
        for xx in range(NX):
            block = tokv[:, pl.ds(pl.multiple_of(zz * 1024 + xx * 256, 256), 256)]
            flip = block.T
            for yy in range(NX):
                at_row = pl.multiple_of(zz * 32, 32)
                tr[0, xx, pl.ds(yy * 256 + at_row, 32), :] = flip[yy * 64:yy * 64 + 32]
                tr[1, yy, pl.ds(xx * 256 + at_row, 32), :] = flip[yy * 64 + 32:yy * 64 + 64]
        return carry

    lax.fori_loop(0, NZ, turn, 0)

    for h in range(HEADS):
        q_s[h * TDEV:(h + 1) * TDEV, :] = rot(
            qkvv[:, h * HD:(h + 1) * HD].astype(F32)).astype(BF)
    loads[1].wait()
    for h in range(HEADS):
        g_s[h * TDEV:(h + 1) * TDEV, :] = gov[:, h * HD:(h + 1) * HD]
    key = lax.broadcasted_iota(jnp.int32, (1, SEQ), 1)
    key_span = key // SPAN
    key_pos = key % SPAN
    for i in range(SPANS):
        key_pos = key_pos + jnp.where(key_span == i, span_s[0, i] * SPAN, 0)
    masked = jnp.where(key_pos <= pos[:, :1], jnp.float32(0.0), jnp.float32(-1e30))
    bias[:TDEV, :] = masked
    bias[TDEV:, :] = masked
    dkt[...] = jnp.zeros_like(dkt)
    dvt[...] = jnp.zeros_like(dvt)

    pl.semaphore_wait(barrier, len(peers))

    own_kv = kv.at[kv_rows, :]
    for off in range(1, NX):
        send(own_kv, own_kv, kvs.at[off - 1], kvr.at[off - 1], dev(z, x, (y + off) % NX, c))
    send(own_kv, own_kv, kvs.at[3], kvr.at[3], partner)

    def slot(m):
        return pl.ds(pl.multiple_of(m * TDEV, TDEV), TDEV)

    gpos = x * (1 - c) + y * c
    opos = y * (1 - c) + x * c
    mine = slot(gpos * 2 + c)
    for off in (2, 1, 3):
        to_x = (x + off) % NX
        to_y = (y + off) % NX
        send(tr.at[0, to_x], at.at[:, slot(x * 2 + c)],
             asnd.at[off - 1], arcv.at[(off - 1) * 2 + c], dev(z, to_x, y, 0))
        send(tr.at[1, to_y], at.at[:, slot(y * 2 + c)],
             asnd.at[off + 2], arcv.at[(off - 1) * 2 + c], dev(z, x, to_y, 1))
    send(tr.at[1 - c, opos], at.at[:, slot(opos * 2 + c)], asnd.at[6], arcv.at[6], partner)
    own_a = pltpu.make_async_copy(tr.at[c, gpos], at.at[:, mine], lsem.at[3])
    own_a.start()

    for off in (1, 3, 2):
        rows_in = slot(((y + NX - off) % NX) * 2 + c)
        got(kv.at[rows_in, :], kvr.at[off - 1])
        send(kv.at[rows_in, :], kv.at[rows_in, :], kvs.at[3 + off], kvr.at[3 + off], partner)
    got(own_kv, kvr.at[3])
    for off in (1, 3, 2):
        got(own_kv, kvr.at[3 + off])

    def heads(n, i, carry):
        pair = n * (PER // 2) + i
        two = pl.ds(pl.multiple_of(pair * 2 * TDEV, 2 * TDEV), 2 * TDEV)
        q2 = q_s[two, :]
        g2 = g_s[two, :]
        keys = kv[:, :HD]
        values = kv[:, HD:]
        s = lax.dot_general(q2, keys, (((1,), (1,)), ((), ())), preferred_element_type=F32)
        s = s * F32(SCALE * LOG2E) + bias[...]
        e = jnp.exp2(s - jnp.max(s, axis=1, keepdims=True))
        p = e * (1.0 / jnp.sum(e, axis=1, keepdims=True))
        pb = p.astype(BF)
        o = jnp.dot(pb, values, preferred_element_type=F32)
        delta = jnp.sum(g2.astype(F32) * o, axis=1, keepdims=True)
        dpr = lax.dot_general(g2, values, (((1,), (1,)), ((), ())), preferred_element_type=F32)
        ds = (p * (dpr - delta)).astype(BF)
        dq = jnp.dot(ds, keys, preferred_element_type=F32) * F32(SCALE)
        for j in range(2):
            g = dq[j * TDEV:(j + 1) * TDEV]
            back = g * cos_s[...] - pltpu.roll(g, HD // 2, 1) * sin_s[...]
            at_col = pl.multiple_of((2 * i + j) * HD, HD)
            bq_own[n, :, pl.ds(at_col, HD)] = back.astype(BF)
        dkt[...] += lax.dot_general(q2, ds, (((0,), (0,)), ((), ())), preferred_element_type=F32)
        dvt[...] += lax.dot_general(g2, pb, (((0,), (0,)), ((), ())), preferred_element_type=F32)
        return carry

    def own_of(ch):
        return bq_own.at[ch] if ch < NQ else bk_own

    def group_of(ch, where):
        return bq.at[ch, where, :] if ch < NQ else bk.at[where, :]

    local = []

    def spread(ch):
        own, base = own_of(ch), 7 * ch
        for k, off in enumerate((1, NX - 1)):
            send(own, group_of(ch, slot(x * 2 + c)), bs.at[base + k],
                 br.at[base + 2 * k + c], dev(z, (x + off) % NX, y, 0))
            send(own, group_of(ch, slot(y * 2 + c)), bs.at[base + 2 + k],
                 br.at[base + 2 * k + c], dev(z, x, (y + off) % NX, 1))
        send(own, group_of(ch, slot(opos * 2 + c)), bs.at[base + 4], br.at[base + 6], partner)
        copy = pltpu.make_async_copy(own, group_of(ch, mine), lsem.at[4 + ch])
        copy.start()
        local.append(copy)

    def beside(step):
        return dev(z, (x + (1 - c) * step) % NX, (y + c * step) % NX, c)

    below = (gpos + NX - 1) % NX
    above = (gpos + 1) % NX

    def relay(ch):
        base = 7 * ch
        up = group_of(ch, slot(below * 2))
        got(up, br.at[base])
        send(up, up, bs.at[base + 5], br.at[base + 4], beside(1))
        down = group_of(ch, slot(above * 2 + 1))
        got(down, br.at[base + 3])
        send(down, down, bs.at[base + 6], br.at[base + 5], beside(NX - 1))

    def rest(ch):
        local[ch].wait()
        for k in (1, 2, 4, 5, 6):
            got(group_of(ch, mine), br.at[7 * ch + k])

    for n in range(NQ):
        lax.fori_loop(0, PER // 2, functools.partial(heads, n), 0)
        if n < NQ - 1:
            spread(n)

    def part(ref, blk):
        return ref[:, pl.ds(pl.multiple_of(blk * TDEV, TDEV), TDEV)]

    for j in range(NX):
        psend[j, :HD, :] = part(dkt, 2 * j + 1 - c).astype(BF)
        psend[j, HD:, :] = part(dvt, 2 * j + 1 - c).astype(BF)
    send(psend, precv, dss.at[3], dsr.at[3], partner)
    got(precv, dsr.at[3])
    for off in range(1, NX):
        to = (y + off) % NX
        blk = 2 * to + c
        dsend[off - 1, :HD, :] = (part(dkt, blk) + precv[to, :HD, :].astype(F32)).astype(BF)
        dsend[off - 1, HD:, :] = (part(dvt, blk) + precv[to, HD:, :].astype(F32)).astype(BF)
        send(dsend.at[off - 1], drecv.at[off - 1], dss.at[off - 1], dsr.at[off - 1],
             dev(z, x, to, c))
    spread(NQ - 1)
    relay(0)

    dk = part(dkt, ctx) + precv[y, :HD, :].astype(F32)
    dv = part(dvt, ctx) + precv[y, HD:, :].astype(F32)
    for off in (1, 3, 2):
        got(drecv.at[off - 1], dsr.at[off - 1])
        dk = dk + drecv[off - 1, :HD, :].astype(F32)
        dv = dv + drecv[off - 1, HD:, :].astype(F32)
    dk = dk.T * F32(SCALE)
    bk_own[:, :HD] = (dk * cos_s[...] - pltpu.roll(dk, HD // 2, 1) * sin_s[...]).astype(BF)
    bk_own[:, HD:] = dv.T.astype(BF)
    spread(NQ)

    def across(step):
        return dev(z, (x + c * step) % NX, (y + (1 - c) * step) % NX, c)

    up_dev, down_dev = across(1), across(NX - 1)

    def term(a, ch):
        lhs = at[pl.ds(pl.multiple_of(a * 256, 256), 256), :]
        rhs = bq[ch] if ch < NQ else bk[...]
        return jnp.dot(lhs, rhs, preferred_element_type=F32)

    def stage(ch, s):
        cols = slice(STARTS[ch], STARTS[ch] + WIDTHS[ch])
        base = ch * 12
        if s == 0:
            y1s[:, cols] = term((opos + 2) % NX, ch).astype(BF)
            send(y1s.at[:128, cols], y1r.at[0, :, cols], cs.at[base], cr.at[base], up_dev)
            send(y1s.at[128:, cols], y1r.at[1, :, cols], cs.at[base + 1], cr.at[base + 1], down_dev)
        elif s == 1:
            t = term((opos + 1) % NX, ch)
            got(y1r.at[0, :, cols], cr.at[base])
            y2s[0, :128, cols] = (t[:128] + y1r[0, :, cols].astype(F32)).astype(BF)
            y2s[0, 128:, cols] = t[128:].astype(BF)
            send(y2s.at[0, :, cols], y2r.at[0, :, cols], cs.at[base + 2], cr.at[base + 2], up_dev)
            t = term((opos + NX - 1) % NX, ch)
            got(y1r.at[1, :, cols], cr.at[base + 1])
            y2s[1, :128, cols] = t[:128].astype(BF)
            y2s[1, 128:, cols] = (t[128:] + y1r[1, :, cols].astype(F32)).astype(BF)
            send(y2s.at[1, :, cols], y2r.at[1, :, cols], cs.at[base + 3], cr.at[base + 3], down_dev)
        elif s == 2:
            cacc[:, cols] = term(opos, ch)
            got(y2r.at[0, :, cols], cr.at[base + 2])
            got(y2r.at[1, :, cols], cr.at[base + 3])
            cacc[:, cols] += y2r[0, :, cols].astype(F32) + y2r[1, :, cols].astype(F32)
            for kind, dist, hop in ((0, 3, 1), (2, 4, 2), (1, 1, 1)):
                for d in range(2):
                    step, jump = (dist, hop) if d == 0 else (NZ - dist, NZ - hop)
                    row = pl.multiple_of(((z + step) % NZ) * 32, 32)
                    size = 32
                    if kind == 2:
                        row, size = row + 16 * d, 16
                    zs[d, kind, :size, cols] = cacc[pl.ds(row, size), cols].astype(BF)
                    sem = base + 4 + 2 * kind + d
                    send(zs.at[d, kind, :size, cols], zr.at[d, kind, :size, cols],
                         cs.at[sem], cr.at[sem], dev((z + jump) % NZ, x, y, c))
        elif s == 3:
            for d in range(2):
                hop = 2 if d == 0 else NZ - 2
                row = pl.multiple_of(((z + hop) % NZ) * 32, 32)
                got(zr.at[d, 0, :, cols], cr.at[base + 4 + d])
                low = cacc[pl.ds(row, 16), cols] + zr[d, 0, :16, cols].astype(F32)
                high = cacc[pl.ds(row + 16, 16), cols] + zr[d, 0, 16:, cols].astype(F32)
                got(zr.at[d, 2, :16, cols], cr.at[base + 8 + d])
                came = zr[d, 2, :16, cols].astype(F32)
                if d == 0:
                    low = low + came
                else:
                    high = high + came
                zs[d, 3, :16, cols] = low.astype(BF)
                zs[d, 3, 16:, cols] = high.astype(BF)
                send(zs.at[d, 3, :, cols], zr.at[d, 3, :, cols],
                     cs.at[base + 10 + d], cr.at[base + 10 + d], dev((z + hop) % NZ, x, y, c))
        else:
            total = cacc[pl.ds(pl.multiple_of(z * 32, 32), 32), cols]
            for kind in (1, 3):
                for d in range(2):
                    got(zr.at[d, kind, :, cols], cr.at[base + 4 + 2 * kind + d])
                    total = total + zr[d, kind, :, cols].astype(F32)
            out_ref[:, cols] = total

    for ch in range(1, NQ):
        relay(ch)
    own_a.wait()
    for k in range(7):
        got(at.at[:, mine], arcv.at[k])
    for t in range(5 + max(LAGS)):
        for ch in reversed(range(NCH)):
            s = t - LAGS[ch]
            if 0 <= s <= 4:
                if s == 0:
                    if ch == NQ:
                        relay(ch)
                    rest(ch)
                stage(ch, s)

    for copy in pending:
        copy.wait_send()


def body(tokens, qkv, grad_out, span_order):
    n_b = 7 * NCH
    n_c = 12 * NCH
    dma = pltpu.SemaphoreType.DMA
    v = pltpu.VMEM
    return pl.pallas_call(
        kernel,
        out_shape=jax.ShapeDtypeStruct((32, 1280), F32),
        in_specs=[pl.BlockSpec(memory_space=pl.ANY)] * 3
        + [pl.BlockSpec(memory_space=pltpu.SMEM)],
        out_specs=pl.BlockSpec(memory_space=pltpu.VMEM),
        scratch_shapes=[
            v((TDEV, 8192), BF), v((TDEV, 1280), BF), v((TDEV, QW), BF),
            v((SEQ, HD), BF), v((SEQ, HD), BF), v((SEQ, 2 * HD), BF),
            v((2 * TDEV, SEQ), F32), v((TDEV, HD), F32), v((TDEV, HD), F32),
            v((HD, SEQ), F32), v((HD, SEQ), F32),
            v((NX, 2 * HD, TDEV), BF), v((NX, 2 * HD, TDEV), BF),
            v((3, 2 * HD, TDEV), BF), v((3, 2 * HD, TDEV), BF),
            v((2, NX, 1024, TDEV), BF), v((1024, SEQ), BF),
            v((NQ, TDEV, QC), BF), v((TDEV, 256), BF), v((NQ, SEQ, QC), BF), v((SEQ, 256), BF),
            v((256, 1280), BF), v((2, 128, 1280), BF),
            v((2, 256, 1280), BF), v((2, 256, 1280), BF),
            v((256, 1280), F32), v((2, 4, 32, 1280), BF), v((2, 4, 32, 1280), BF),
            dma((4 + NCH,)), dma((7,)), dma((7,)), dma((7,)), dma((7,)), dma((4,)), dma((4,)),
            dma((n_b,)), dma((n_b,)), dma((n_c,)), dma((n_c,)),
        ],
        compiler_params=pltpu.CompilerParams(collective_id=0, has_side_effects=True),
    )(tokens, qkv, grad_out, span_order)


def solution(mesh):
    return jax.shard_map(
        body,
        mesh=mesh,
        in_specs=(
            P(("dp", "ctx"), None),
            P(("dp", "ctx"), None),
            P(("dp", "ctx"), None),
            P("dp", None),
        ),
        out_specs=P(("dp", "ctx"), None),
        check_vma=False,
    )
```

time: 76.3 us -> 67.7 us (0.89)
  the two profiles are of different devices: /device:TPU:9 before, /device:TPU:1 now
where the time goes in v2:
time: 67.7 us; the launch traced here: 67.4 us
  Pallas kernels  65.8 us (97%)
  local copies, waits for them, and re-layouts  1.59 us (2%)
    pallas_call x1, Pallas kernels, body(): pl.pallas_call(kernel, out_shape=jax.ShapeDtypeStruct((32, 1280), F32), i...  65.8 us
    unnamed x1, local copies, waits for them, and re-layouts  1.59 us

profile of v2, /device:TPU:1, one launch (start us, length us, event | category | flops | bytes accessed | tf_op | source)
XLA Modules:
  0.0 67.4 jit_solution(7136935123721712361)
XLA Ops:
  0.0 65.8 %shard_map.46 = f32[32,1280]{1,0:T(8,128)} custom-call(bf16[128,8192]{1,0:T(8,128)(2,1)} %tok_h.1, bf16[128,1280]{1,0:T(8,128)(2,1)} %qkv_h.1, bf16[128,1024]{1,0:T(8,128)(2,1)} %go_h.1, s32[1,16]{1,0:T(1,128)} %span_s.1), custom_call_target="tpu_custom_call" | custom-call | tf_op jit(solution)/shard_map/pallas_call | solution.py:365
  65.8 1.6 %copy.6 = f32[32,1280]{1,0:T(8,128)} copy(f32[32,1280]{1,0:T(8,128)} %shard_map.46) | data formatting | bytes 327680

commit v3 on v2

--- a/solution.py
+++ b/solution.py
@@ -29,13 +29,20 @@
 WIDTHS = (QC,) * NQ + (2 * HD,)
 STARTS = tuple(QC * i for i in range(NQ)) + (QW,)
 NCH = NQ + 1
-LAGS = (0, 1, 2)
+GATHER_DIRECT = ()
+FIRST_DIRECT = ()
+Z_DIRECT = (2,)
+FAR_AT = (0, 1)
+ORDER = (
+    "P", "S1", "R0", "D", "S2", "R1", "A", "G0", "F0", "R2", "G1", "F1", "N0",
+    "G2", "F2", "N1", "Y0", "N2", "Y1", "Z0", "Y2", "Z1", "O0", "Z2", "O1", "O2",
+)
 
 
 def kernel(
     tok_h, qkv_h, go_h, span_s, out_ref,
     tokv, qkvv, gov, q_s, g_s, kv, bias, cos_s, sin_s, dkt, dvt, psend, precv, dsend, drecv,
-    tr, at, bq_own, bk_own, bq, bk, y1s, y1r, y2s, y2r, cacc, zs, zr,
+    tr, at, bq_own, bk_own, bq, bk, y1s, y1r, y2s, y2r, cacc, zs, zr, zd,
     lsem, kvs, kvr, asnd, arcv, dss, dsr, bs, br, cs, cr,
 ):
     dp = lax.axis_index("dp")
@@ -75,7 +82,7 @@
         load.start()
 
     barrier = pltpu.get_barrier_semaphore()
-    peers = [dev((z + off) % NZ, x, y, c) for off in (1, 7, 2, 6)]
+    peers = [dev((z + off) % NZ, x, y, c) for off in ((1, 7, 2, 6, 3, 5, 4) if Z_DIRECT else (1, 7, 2, 6))]
     for off in range(1, NX):
         for cc in range(2):
             peers.append(dev(z, x, (y + off) % NX, cc))
@@ -150,13 +157,25 @@
     gpos = x * (1 - c) + y * c
     opos = y * (1 - c) + x * c
     mine = slot(gpos * 2 + c)
-    for off in (2, 1, 3):
+    for off in (1, 3):
         to_x = (x + off) % NX
         to_y = (y + off) % NX
         send(tr.at[0, to_x], at.at[:, slot(x * 2 + c)],
              asnd.at[off - 1], arcv.at[(off - 1) * 2 + c], dev(z, to_x, y, 0))
         send(tr.at[1, to_y], at.at[:, slot(y * 2 + c)],
              asnd.at[off + 2], arcv.at[(off - 1) * 2 + c], dev(z, x, to_y, 1))
+
+    def far_tokens(place):
+        for n in range(2):
+            if FAR_AT[n] == place:
+                half = slice(512 * n, 512 * n + 512)
+                to_x = (x + 2) % NX
+                to_y = (y + 2) % NX
+                send(tr.at[0, to_x, half], at.at[half, slot(x * 2 + c)],
+                     asnd.at[1 + 6 * n], arcv.at[2 + 5 * n + c], dev(z, to_x, y, 0))
+                send(tr.at[1, to_y, half], at.at[half, slot(y * 2 + c)],
+                     asnd.at[4 + 4 * n], arcv.at[2 + 5 * n + c], dev(z, x, to_y, 1))
+
     send(tr.at[1 - c, opos], at.at[:, slot(opos * 2 + c)], asnd.at[6], arcv.at[6], partner)
     own_a = pltpu.make_async_copy(tr.at[c, gpos], at.at[:, mine], lsem.at[3])
     own_a.start()
@@ -168,6 +187,8 @@
     got(own_kv, kvr.at[3])
     for off in (1, 3, 2):
         got(own_kv, kvr.at[3 + off])
+
+    far_tokens(0)
 
     def heads(n, i, carry):
         pair = n * (PER // 2) + i
@@ -205,12 +226,13 @@
 
     def spread(ch):
         own, base = own_of(ch), 7 * ch
-        for k, off in enumerate((1, NX - 1)):
-            send(own, group_of(ch, slot(x * 2 + c)), bs.at[base + k],
+        hops = (1, NX - 1, 2) if ch in GATHER_DIRECT else (1, NX - 1)
+        for k, off in enumerate(hops):
+            send(own, group_of(ch, slot(x * 2 + c)), bs.at[base + 2 * k],
                  br.at[base + 2 * k + c], dev(z, (x + off) % NX, y, 0))
-            send(own, group_of(ch, slot(y * 2 + c)), bs.at[base + 2 + k],
+            send(own, group_of(ch, slot(y * 2 + c)), bs.at[base + 2 * k + 1],
                  br.at[base + 2 * k + c], dev(z, x, (y + off) % NX, 1))
-        send(own, group_of(ch, slot(opos * 2 + c)), bs.at[base + 4], br.at[base + 6], partner)
+        send(own, group_of(ch, slot(opos * 2 + c)), bs.at[base + 6], br.at[base + 6], partner)
         copy = pltpu.make_async_copy(own, group_of(ch, mine), lsem.at[4 + ch])
         copy.start()
         local.append(copy)
@@ -222,52 +244,62 @@
     above = (gpos + 1) % NX
 
     def relay(ch):
+        if ch in GATHER_DIRECT:
+            return
         base = 7 * ch
         up = group_of(ch, slot(below * 2))
         got(up, br.at[base])
-        send(up, up, bs.at[base + 5], br.at[base + 4], beside(1))
+        send(up, up, bs.at[base + 4], br.at[base + 4], beside(1))
         down = group_of(ch, slot(above * 2 + 1))
         got(down, br.at[base + 3])
-        send(down, down, bs.at[base + 6], br.at[base + 5], beside(NX - 1))
+        send(down, down, bs.at[base + 5], br.at[base + 5], beside(NX - 1))
 
     def rest(ch):
         local[ch].wait()
-        for k in (1, 2, 4, 5, 6):
+        for k in range(7) if ch in GATHER_DIRECT else (1, 2, 4, 5, 6):
             got(group_of(ch, mine), br.at[7 * ch + k])
 
     for n in range(NQ):
         lax.fori_loop(0, PER // 2, functools.partial(heads, n), 0)
         if n < NQ - 1:
             spread(n)
+    far_tokens(1)
 
     def part(ref, blk):
         return ref[:, pl.ds(pl.multiple_of(blk * TDEV, TDEV), TDEV)]
 
-    for j in range(NX):
-        psend[j, :HD, :] = part(dkt, 2 * j + 1 - c).astype(BF)
-        psend[j, HD:, :] = part(dvt, 2 * j + 1 - c).astype(BF)
-    send(psend, precv, dss.at[3], dsr.at[3], partner)
-    got(precv, dsr.at[3])
-    for off in range(1, NX):
-        to = (y + off) % NX
-        blk = 2 * to + c
-        dsend[off - 1, :HD, :] = (part(dkt, blk) + precv[to, :HD, :].astype(F32)).astype(BF)
-        dsend[off - 1, HD:, :] = (part(dvt, blk) + precv[to, HD:, :].astype(F32)).astype(BF)
-        send(dsend.at[off - 1], drecv.at[off - 1], dss.at[off - 1], dsr.at[off - 1],
-             dev(z, x, to, c))
-    spread(NQ - 1)
-    relay(0)
-
-    dk = part(dkt, ctx) + precv[y, :HD, :].astype(F32)
-    dv = part(dvt, ctx) + precv[y, HD:, :].astype(F32)
-    for off in (1, 3, 2):
-        got(drecv.at[off - 1], dsr.at[off - 1])
-        dk = dk + drecv[off - 1, :HD, :].astype(F32)
-        dv = dv + drecv[off - 1, HD:, :].astype(F32)
-    dk = dk.T * F32(SCALE)
-    bk_own[:, :HD] = (dk * cos_s[...] - pltpu.roll(dk, HD // 2, 1) * sin_s[...]).astype(BF)
-    bk_own[:, HD:] = dv.T.astype(BF)
-    spread(NQ)
+    def chip_sum():
+        for j in range(NX):
+            psend[j, :HD, :] = part(dkt, 2 * j + 1 - c).astype(BF)
+            psend[j, HD:, :] = part(dvt, 2 * j + 1 - c).astype(BF)
+        send(psend, precv, dss.at[3], dsr.at[3], partner)
+        got(precv, dsr.at[3])
+        for off in range(1, NX):
+            to = (y + off) % NX
+            blk = 2 * to + c
+            dsend[off - 1, :HD, :] = (part(dkt, blk) + precv[to, :HD, :].astype(F32)).astype(BF)
+            dsend[off - 1, HD:, :] = (part(dvt, blk) + precv[to, HD:, :].astype(F32)).astype(BF)
+            send(dsend.at[off - 1], drecv.at[off - 1], dss.at[off - 1], dsr.at[off - 1],
+                 dev(z, x, to, c))
+
+    def key_value_grads():
+        dk = part(dkt, ctx) + precv[y, :HD, :].astype(F32)
+        dv = part(dvt, ctx) + precv[y, HD:, :].astype(F32)
+        for off in (1, 3, 2):
+            got(drecv.at[off - 1], dsr.at[off - 1])
+            dk = dk + drecv[off - 1, :HD, :].astype(F32)
+            dv = dv + drecv[off - 1, HD:, :].astype(F32)
+        dk = dk.T * F32(SCALE)
+        bk_own[:, :HD] = (dk * cos_s[...] - pltpu.roll(dk, HD // 2, 1) * sin_s[...]).astype(BF)
+        bk_own[:, HD:] = dv.T.astype(BF)
+
+    def tokens_in():
+        own_a.wait()
+        for k in (0, 1, 4, 5, 6):
+            got(at.at[:, mine], arcv.at[k])
+        for k in (2, 3, 7, 8):
+            got(at.at[:512, mine], arcv.at[k])
+
 
     def across(step):
         return dev(z, (x + c * step) % NX, (y + (1 - c) * step) % NX, c)
@@ -282,26 +314,50 @@
     def stage(ch, s):
         cols = slice(STARTS[ch], STARTS[ch] + WIDTHS[ch])
         base = ch * 12
-        if s == 0:
+        if s == 0 and ch in FIRST_DIRECT:
+            for d, (blk, to) in enumerate(((opos + 1, up_dev), (opos + NX - 1, down_dev))):
+                y2s[d, :, cols] = term(blk % NX, ch).astype(BF)
+                send(y2s.at[d, :, cols], y2r.at[d, :, cols],
+                     cs.at[base + 2 + d], cr.at[base + 2 + d], to)
+            y1s[:, cols] = term((opos + 2) % NX, ch).astype(BF)
+            for d in range(2):
+                send(y1s.at[128 * d:128 * d + 128, cols], y1r.at[d, :, cols],
+                     cs.at[base + d], cr.at[base + d], across(2))
+        elif s == 1 and ch in FIRST_DIRECT:
+            cacc[:, cols] = term(opos, ch)
+        elif s == 0:
             y1s[:, cols] = term((opos + 2) % NX, ch).astype(BF)
             send(y1s.at[:128, cols], y1r.at[0, :, cols], cs.at[base], cr.at[base], up_dev)
             send(y1s.at[128:, cols], y1r.at[1, :, cols], cs.at[base + 1], cr.at[base + 1], down_dev)
         elif s == 1:
             t = term((opos + 1) % NX, ch)
+            u = term((opos + NX - 1) % NX, ch)
             got(y1r.at[0, :, cols], cr.at[base])
             y2s[0, :128, cols] = (t[:128] + y1r[0, :, cols].astype(F32)).astype(BF)
             y2s[0, 128:, cols] = t[128:].astype(BF)
             send(y2s.at[0, :, cols], y2r.at[0, :, cols], cs.at[base + 2], cr.at[base + 2], up_dev)
-            t = term((opos + NX - 1) % NX, ch)
             got(y1r.at[1, :, cols], cr.at[base + 1])
-            y2s[1, :128, cols] = t[:128].astype(BF)
-            y2s[1, 128:, cols] = (t[128:] + y1r[1, :, cols].astype(F32)).astype(BF)
+            y2s[1, :128, cols] = u[:128].astype(BF)
+            y2s[1, 128:, cols] = (u[128:] + y1r[1, :, cols].astype(F32)).astype(BF)
             send(y2s.at[1, :, cols], y2r.at[1, :, cols], cs.at[base + 3], cr.at[base + 3], down_dev)
+            cacc[:, cols] = term(opos, ch)
         elif s == 2:
-            cacc[:, cols] = term(opos, ch)
             got(y2r.at[0, :, cols], cr.at[base + 2])
             got(y2r.at[1, :, cols], cr.at[base + 3])
             cacc[:, cols] += y2r[0, :, cols].astype(F32) + y2r[1, :, cols].astype(F32)
+            if ch in FIRST_DIRECT:
+                for d in range(2):
+                    half = slice(128 * d, 128 * d + 128)
+                    got(y1r.at[d, :, cols], cr.at[base + d])
+                    cacc[half, cols] += y1r[d, :, cols].astype(F32)
+            if ch in Z_DIRECT:
+                for k, hop in enumerate((4, 3, 5, 2, 6, 1, 7)):
+                    to = (z + hop) % NZ
+                    row = pl.multiple_of(to * 32, 32)
+                    zd[0, k, :, cols] = cacc[pl.ds(row, 32), cols].astype(BF)
+                    send(zd.at[0, k, :, cols], zd.at[1, k, :, cols], cs.at[base + 4 + k], cr.at[base + 4 + k],
+                         dev(to, x, y, c))
+                return
             for kind, dist, hop in ((0, 3, 1), (2, 4, 2), (1, 1, 1)):
                 for d in range(2):
                     step, jump = (dist, hop) if d == 0 else (NZ - dist, NZ - hop)
@@ -313,6 +369,14 @@
                     sem = base + 4 + 2 * kind + d
                     send(zs.at[d, kind, :size, cols], zr.at[d, kind, :size, cols],
                          cs.at[sem], cr.at[sem], dev((z + jump) % NZ, x, y, c))
+        elif s == 3 and ch in Z_DIRECT:
+            pass
+        elif s == 4 and ch in Z_DIRECT:
+            total = cacc[pl.ds(pl.multiple_of(z * 32, 32), 32), cols]
+            for k in range(7):
+                got(zd.at[1, k, :, cols], cr.at[base + 4 + k])
+                total = total + zd[1, k, :, cols].astype(F32)
+            out_ref[:, cols] = total
         elif s == 3:
             for d in range(2):
                 hop = 2 if d == 0 else NZ - 2
@@ -338,20 +402,18 @@
                     total = total + zr[d, kind, :, cols].astype(F32)
             out_ref[:, cols] = total
 
-    for ch in range(1, NQ):
-        relay(ch)
-    own_a.wait()
-    for k in range(7):
-        got(at.at[:, mine], arcv.at[k])
-    for t in range(5 + max(LAGS)):
-        for ch in reversed(range(NCH)):
-            s = t - LAGS[ch]
-            if 0 <= s <= 4:
-                if s == 0:
-                    if ch == NQ:
-                        relay(ch)
-                    rest(ch)
-                stage(ch, s)
+    for op in ORDER:
+        ch = int(op[1:] or 0)
+        if op == "P":
+            chip_sum()
+        elif op == "D":
+            key_value_grads()
+        elif op == "A":
+            tokens_in()
+        elif op[0] in "SRG":
+            {"S": spread, "R": relay, "G": rest}[op[0]](ch)
+        else:
+            stage(ch, "FNYZO".index(op[0]))
 
     for copy in pending:
         copy.wait_send()
@@ -379,8 +441,8 @@
             v((NQ, TDEV, QC), BF), v((TDEV, 256), BF), v((NQ, SEQ, QC), BF), v((SEQ, 256), BF),
             v((256, 1280), BF), v((2, 128, 1280), BF),
             v((2, 256, 1280), BF), v((2, 256, 1280), BF),
-            v((256, 1280), F32), v((2, 4, 32, 1280), BF), v((2, 4, 32, 1280), BF),
-            dma((4 + NCH,)), dma((7,)), dma((7,)), dma((7,)), dma((7,)), dma((4,)), dma((4,)),
+            v((256, 1280), F32), v((2, 4, 32, 1280), BF), v((2, 4, 32, 1280), BF), v((2, 7, 32, 1280), BF),
+            dma((4 + NCH,)), dma((7,)), dma((7,)), dma((9,)), dma((9,)), dma((4,)), dma((4,)),
             dma((n_b,)), dma((n_b,)), dma((n_c,)), dma((n_c,)),
         ],
         compiler_params=pltpu.CompilerParams(collective_id=0, has_side_effects=True),

time: 67.7 us -> 65.7 us (0.970)
  Pallas kernels: 65.8 us -> 64 us
    pallas_call x1, Pallas kernels: 65.8 us -> 64 us  [body(): pl.pallas_call(kernel, out_shape=jax.ShapeDtypeStruct((32, 1280), F32), i...]
where the time goes in v3:
time: 65.7 us; the launch traced here: 65.6 us
  Pallas kernels  64 us (97%)
  local copies, waits for them, and re-layouts  1.59 us (2%)
    pallas_call x1, Pallas kernels, body(): pl.pallas_call(kernel, out_shape=jax.ShapeDtypeStruct((32, 1280), F32), i...  64 us
    unnamed x1, local copies, waits for them, and re-layouts  1.59 us

profile of v3, /device:TPU:1, one launch (start us, length us, event | category | flops | bytes accessed | tf_op | source)
XLA Modules:
  0.0 65.6 jit_solution(7677751285831463394)
XLA Ops:
  0.0 64.0 %shard_map.46 = f32[32,1280]{1,0:T(8,128)} custom-call(bf16[128,8192]{1,0:T(8,128)(2,1)} %tok_h.1, bf16[128,1280]{1,0:T(8,128)(2,1)} %qkv_h.1, bf16[128,1024]{1,0:T(8,128)(2,1)} %go_h.1, s32[1,16]{1,0:T(1,128)} %span_s.1), custom_call_target="tpu_custom_call" | custom-call | tf_op jit(solution)/shard_map/pallas_call | solution.py:427
  64.0 1.6 %copy.6 = f32[32,1280]{1,0:T(8,128)} copy(f32[32,1280]{1,0:T(8,128)} %shard_map.46) | data formatting | bytes 327680

commit v4 on v3

--- a/solution.py
+++ b/solution.py
@@ -31,7 +31,7 @@
 NCH = NQ + 1
 GATHER_DIRECT = ()
 FIRST_DIRECT = ()
-Z_DIRECT = (2,)
+Z_DIRECT = (0, 2)
 FAR_AT = (0, 1)
 ORDER = (
     "P", "S1", "R0", "D", "S2", "R1", "A", "G0", "F0", "R2", "G1", "F1", "N0",

time: 65.7 us -> 65.6 us (level)
  no operation moved by 1% of the time
where the time goes in v4:
time: 65.6 us; the launch traced here: 65.5 us
  Pallas kernels  63.9 us (97%)
  local copies, waits for them, and re-layouts  1.59 us (2%)
    pallas_call x1, Pallas kernels, body(): pl.pallas_call(kernel, out_shape=jax.ShapeDtypeStruct((32, 1280), F32), i...  63.9 us
    unnamed x1, local copies, waits for them, and re-layouts  1.59 us

profile of v4, /device:TPU:1, one launch (start us, length us, event | category | flops | bytes accessed | tf_op | source)
XLA Modules:
  0.0 65.5 jit_solution(15525294939435717976)
XLA Ops:
  0.0 63.9 %shard_map.46 = f32[32,1280]{1,0:T(8,128)} custom-call(bf16[128,8192]{1,0:T(8,128)(2,1)} %tok_h.1, bf16[128,1280]{1,0:T(8,128)(2,1)} %qkv_h.1, bf16[128,1024]{1,0:T(8,128)(2,1)} %go_h.1, s32[1,16]{1,0:T(1,128)} %span_s.1), custom_call_target="tpu_custom_call" | custom-call | tf_op jit(solution)/shard_map/pallas_call | solution.py:427
  63.9 1.6 %copy.6 = f32[32,1280]{1,0:T(8,128)} copy(f32[32,1280]{1,0:T(8,128)} %shard_map.46) | data formatting | bytes 327680
